TPU v7x, 256 devices: a whole 4x4x8 slice. The times are simulated.
256 devices in a mesh: row: 16 (over z_lo, x, core), col: 4 (over y), item: 4 (over z_hi).
Axes of the slice: x: 4, y: 4, z: 8 (z_hi: 4, z_lo: 2; z = z_hi * 2 + z_lo), core: 2. Of those that a mesh axis runs over, the one named last changes fastest.
Arguments:
- tokens: bfloat16 [4, 16, 64, 2432], P('item', 'row', 'col'), may hold values from -6 to 6
- text_keys_values: bfloat16 [4, 154, 2, 2048], P('item', None, None, 'row'), may hold values from -200 to 200
- text_length: int32 [4], P('item'), may hold values from 2 to 154, as said below
- modulation: float32 [4, 8, 2432], P('item'), may hold values from -4 to 4
- input_weight: bfloat16 [2432, 3, 2048], P(None, None, 'row'), may hold values from -0.125 to 0.125
- norm_gain: float32 [2, 64], replicated, may hold values from 1 to 3
- output_weight: bfloat16 [2048, 2432], P('row'), may hold values from -0.125 to 0.125
- up_weight: bfloat16 [2432, 9728], P(None, 'row'), may hold values from -0.125 to 0.125
- down_weight: bfloat16 [9728, 2432], P('row'), may hold values from -0.0625 to 0.0625
- final_weight: bfloat16 [2432, 64], replicated, may hold values from -0.125 to 0.125
- step_index: int32 [1], replicated, may hold values from 0 to 27
- latent: float32 [4, 16, 4096], P('item', 'row', 'col'), may hold values from -6 to 6
Outputs:
- tokens_out: bfloat16 [4, 16, 64, 2432], P('item', 'row', 'col')
- velocity: float32 [4, 16, 4096], P('item', 'row', 'col')
- latent_next: float32 [4, 16, 4096], P('item', 'row', 'col')
Inputs may be any that keep to these rules, and one draw needn't show every extreme that they name: `text_length`: at least one sequence has all 154 text tokens valid.
All inputs are finite; a program needn't handle non-finite values.
Results may differ from a plain program's by a relative error of at most 0.024.
Values may be sent and summed in bfloat16 or wider, within the bound.
A program may use at most 64 MiB of HBM per device.

v0:
```python
import jax
import jax.numpy as jnp
from jax import lax
from jax.sharding import PartitionSpec as P

HD = 64
STEPS = 28
EPSILON = 1e-06
SHIFT_FACTOR = 3.0
GUIDANCE = 4.5
MASKED = -1e30


def partner_2(value, axis, apart):
    mask = 2**apart
    pairs = [(source, source ^ mask) for source in range(lax.axis_size(axis))]
    return lax.ppermute(value, axis, pairs)


def layer_norm(values):
    center = values - jnp.mean(values, axis=-1, keepdims=True)
    spread = jnp.mean(center * center, axis=-1, keepdims=True)
    return center * lax.rsqrt(spread + EPSILON)


def modulate(values, shift_term, scale_term):
    return (layer_norm(values) * (1.0 + scale_term) + shift_term).astype(jnp.bfloat16)


def root_norm(values, gain_row):
    return (
        values * lax.rsqrt(jnp.mean(values * values, axis=-1, keepdims=True) + EPSILON) * gain_row
    )


def noise_level(position):
    linear = 1.0 - position / STEPS
    return SHIFT_FACTOR * linear / (1.0 + (SHIFT_FACTOR - 1.0) * linear)


def on_device(
    tokens,
    text_keys_values,
    text_length,
    modulation,
    input_weight,
    norm_gain,
    output_weight,
    up_weight,
    down_weight,
    final_weight,
    step_index,
    latent,
):
    tile_rows = tokens.shape[1] * tokens.shape[2]
    model_width = tokens.shape[3]
    mod_rows = modulation[0]
    row_position = lax.axis_index("row")
    stripe_tokens = lax.all_gather(tokens, "row", axis=1, tiled=True)
    stripe_states = stripe_tokens.reshape(-1, model_width).astype(jnp.float32)
    stripe_rows = stripe_states.shape[0]
    local_width = input_weight.shape[2]
    local_heads = local_width // HD
    attn_input = modulate(stripe_states, mod_rows[0], mod_rows[1])
    projected = jnp.dot(
        attn_input,
        input_weight.reshape(model_width, 3 * local_width),
        preferred_element_type=jnp.float32,
    )
    projected = projected.reshape(stripe_rows, 3, local_heads, HD)
    queries = root_norm(projected[:, 0], norm_gain[0]).astype(jnp.bfloat16).transpose(1, 0, 2)
    keys_image = (
        root_norm(projected[:, 1], norm_gain[1])
        .astype(jnp.bfloat16)
        .reshape(stripe_rows, local_width)
    )
    values_image = projected[:, 2].astype(jnp.bfloat16).reshape(stripe_rows, local_width)
    text_pairs = text_keys_values[0]
    keys_text = text_pairs[:, 0].reshape(-1, local_heads, HD)
    values_text = text_pairs[:, 1].reshape(-1, local_heads, HD)
    text_valid = jnp.arange(keys_text.shape[0]) < text_length[0]
    text_scores = jnp.einsum(
        "hsd,thd->hst", queries, keys_text, preferred_element_type=jnp.float32
    ) * HD ** (-0.5)
    text_scores = jnp.where(text_valid[None, None, :], text_scores, MASKED)
    largest = jnp.max(text_scores, axis=-1)
    text_weights = jnp.exp(text_scores - largest[..., None])
    total_mass = jnp.sum(text_weights, axis=-1)
    weighted = jnp.einsum(
        "hst,thd->hsd",
        text_weights.astype(jnp.bfloat16),
        values_text,
        preferred_element_type=jnp.float32,
    )

    def one_block(running, block_pair):
        running_max, running_mass, running_sum = running
        key_block, value_block = block_pair
        scores = jnp.einsum(
            "hsd,khd->hsk", queries, key_block, preferred_element_type=jnp.float32
        ) * HD ** (-0.5)
        new_max = jnp.maximum(running_max, jnp.max(scores, axis=-1))
        factor = jnp.exp(running_max - new_max)
        weights = jnp.exp(scores - new_max[..., None])
        new_mass = running_mass * factor + jnp.sum(weights, axis=-1)
        new_sum = running_sum * factor[..., None] + jnp.einsum(
            "hsk,khd->hsd",
            weights.astype(jnp.bfloat16),
            value_block,
            preferred_element_type=jnp.float32,
        )
        return ((new_max, new_mass, new_sum), None)

    key_piece = lax.all_gather(keys_image, "col", axis=0, tiled=True)
    value_piece = lax.all_gather(values_image, "col", axis=0, tiled=True)
    blocks = key_piece.shape[0] // stripe_rows
    key_blocks = key_piece.reshape(blocks, stripe_rows, local_heads, HD)
    value_blocks = value_piece.reshape(blocks, stripe_rows, local_heads, HD)
    result, unused = lax.scan(
        one_block, (largest, total_mass, weighted), (key_blocks, value_blocks)
    )
    largest, total_mass, weighted = result
    attended = (
        (weighted / total_mass[..., None])
        .astype(jnp.bfloat16)
        .transpose(1, 0, 2)
        .reshape(stripe_rows, local_width)
    )
    attention = lax.psum(
        jnp.dot(attended, output_weight, preferred_element_type=jnp.float32).astype(jnp.bfloat16),
        "row",
    ).astype(jnp.float32)
    stripe_middle = stripe_states + mod_rows[2] * attention
    feed_input = modulate(stripe_middle, mod_rows[3], mod_rows[4])
    hidden = jax.nn.gelu(
        jnp.dot(feed_input, up_weight, preferred_element_type=jnp.float32), approximate=True
    ).astype(jnp.bfloat16)
    middle = lax.dynamic_slice_in_dim(stripe_middle, row_position * tile_rows, tile_rows, 0)
    feed = lax.psum_scatter(
        jnp.dot(hidden, down_weight, preferred_element_type=jnp.float32).astype(jnp.bfloat16),
        "row",
        scatter_dimension=0,
        tiled=True,
    ).astype(jnp.float32)
    leaving = middle + mod_rows[5] * feed
    tokens_out = leaving.astype(jnp.bfloat16).reshape(tokens.shape)
    final_input = modulate(leaving, mod_rows[6], mod_rows[7])
    raw_velocity = jnp.dot(final_input, final_weight, preferred_element_type=jnp.float32).reshape(
        1, tokens.shape[1], -1
    )
    partner = partner_2(raw_velocity, "item", 0)
    is_guided = lax.axis_index("item") % 2 == 0
    guided = jnp.where(is_guided, raw_velocity, partner)
    unguided = jnp.where(is_guided, partner, raw_velocity)
    velocity = unguided + GUIDANCE * (guided - unguided)
    position = step_index[0].astype(jnp.float32)
    step_size = noise_level(position + 1.0) - noise_level(position)
    return (tokens_out, velocity, latent + step_size * velocity)


def solution(mesh):
    in_specs = (
        P("item", "row", "col", None),
        P("item", None, None, "row"),
        P("item"),
        P("item", None, None),
        P(None, None, "row"),
        P(),
        P("row", None),
        P(None, "row"),
        P("row", None),
        P(),
        P(),
        P("item", "row", "col"),
    )
    out_specs = (P("item", "row", "col", None), P("item", "row", "col"), P("item", "row", "col"))
    return jax.shard_map(
        on_device, mesh=mesh, in_specs=in_specs, out_specs=out_specs, check_vma=False
    )
```

profile of v0, /device:TPU:8, one launch (start us, length us, event | category | flops | bytes accessed | tf_op | source)
XLA Modules:
  0.0 311.7 jit_solution(12788335768457517483)
XLA Ops:
  7.2 0.0 copy-start
  7.2 0.0 all-gather.2.cloned.1.call-start
  7.3 0.7 all-gather.2.cloned.1.call-update
  7.9 0.0 all-reduce.2.cloned.1.call-start
  8.0 4.1 %copy.26 = bf16[2432,3,128]{0,2,1:T(8,128)(2,1)} copy(bf16[2432,3,128]{2,0,1:T(8,128)(2,1)} %param.18) | data formatting | bytes 3735552 | tf_op args[4]
  12.1 0.1 fusion.53
  12.2 0.1 copy.27
  13.0 0.1 copy.28
  13.1 0.1 mul.229
  13.2 0.7 add_reduce_fusion
  13.9 34.3 %all-gather.2.cloned.1.call-done = bf16[1,16,16,2432]{3,2,0,1:T(8,128)(2,1)} async-done(((bf16[1,1,16,2432]{3,2,0,1:T(8,128)(2,1)}), bf16[1,16,16,2432]{3,2,0,1:T(8,128)(2,1)}) %all-gather.2.cloned.1.call-update) | async-done | bytes 1245200 | tf_op jit(solution)/shard_map/all_gather | solution.py:59
  48.2 1.7 convert_reduce_fusion
  49.9 1.7 multiply_reduce_fusion.1
  51.7 0.0 copy-done.1
  51.7 0.6 add_convert_fusion.1
  52.3 0.0 copy-done.3
  52.3 0.7 fusion.55
  53.1 0.1 fusion.41
  53.2 0.3 fusion.54
  53.4 0.1 fusion.30
  53.5 0.2 fusion.31
  53.7 0.1 fusion.35
  53.8 12.6 %all_gather.10 = bf16[1024,128]{0,1:T(8,128)(2,1)S(1)} all-gather(bf16[256,128]{0,1:T(8,128)(2,1)S(1)} %fusion.35), channel_id=1, replica_groups=mesh['row'=16,'col'=4,'item'=4] {'col'}, dimensions={0}, use_global_device_ids=true | all-gather | bytes 327680 | tf_op jit(solution)/shard_map/all_gather | solution.py:114
  66.4 0.9 reshape.190
  67.3 1.0 copy.29
  68.3 13.0 %all_gather.11 = bf16[1024,128]{0,1:T(8,128)(2,1)} all-gather(bf16[256,128]{0,1:T(8,128)(2,1)S(1)} %bitcast.82), channel_id=1, replica_groups=mesh['row'=16,'col'=4,'item'=4] {'col'}, dimensions={0}, use_global_device_ids=true | all-gather | bytes 327680 | tf_op jit(solution)/shard_map/all_gather | solution.py:115
  81.3 1.8 reshape.191
  83.1 1.7 copy.30
  84.8 6.1 %while.14 = (s32[]{:T(128)}, f32[2,256]{1,0:T(2,128)S(1)}, f32[2,256]{1,0:T(2,128)S(1)}, f32[2,256,64]{1,2,0:T(8,128)S(1)}, bf16[4,256,2,64]{1,3,2,0:T(8,128)(2,...) while((s32[]{:T(128)}, f32[2,256]{1,0:T(2,128)S(1)}, ...), condition=%wide.region_9.10_spmd, body=%wide.region_6.9_spmd.sunk | while | flops 34407424 | bytes 2064985 | solution.py:119
  84.8 0.3 fusion.75
  85.1 0.1 fusion.76
  85.2 1.1 convolution_add_fusion.2
  86.3 0.3 fusion.75
  86.7 0.1 fusion.76
  86.8 1.1 convolution_add_fusion.2
  87.9 0.3 fusion.75
  88.2 0.1 fusion.76
  88.3 1.1 convolution_add_fusion.2
  89.4 0.3 fusion.75
  89.7 0.1 fusion.76
  89.8 1.1 convolution_add_fusion.2
  91.0 2.7 convolution_convert_fusion
  93.6 0.0 all-reduce.2.cloned.1.call-update
  93.6 0.0 reduce-scatter.2.cloned.1.call-start
  93.7 124.3 %all-reduce.2.cloned.1.call-done = bf16[256,2432]{1,0:T(8,128)(2,1)} async-done(((bf16[256,2432]{1,0:T(8,128)(2,1)}), bf16[256,2432]{1,0:T(8,128)(2,1)}) %all-reduce.2.cloned.1.call-update) | async-done | bytes 1245200 | tf_op jit(solution)/shard_map/psum | solution.py:129
  218.0 2.2 fusion.51
  220.2 0.0 copy-start.7
  220.2 1.4 copy-done.2
  221.6 0.4 multiply_reduce_fusion
  222.0 0.0 copy-done
  222.0 0.0 copy-done.7
  222.0 0.0 copy-start.5
  222.0 7.5 %convolution_convert_fusion.1 = bf16[256,2432]{1,0:T(8,128)(2,1)} fusion(bf16[608,2432]{1,0:T(8,128)(2,1)S(1)} %copy-done, bf16[2432,608]{0,1:T(8,128)(2,1)} %param.21, f32[256,2432]{1,0:T(8,128)} %copy-done.2, f32[2432]{0:T(1024)S(1)} %get-tuple-element.58, f32[2432]{0:T(1024)S(1)} %copy-done.7, f32[256]{0:T(256)S(1)} %add_rsqrt_fusion.3, ...), kind=kOutput, calls=%fused_computation.16 | convolution fusion | flops 1519280128 | bytes 9671680 | tf_op jit(solution)/shard_map/dot_general | solution.py:140
  229.5 0.0 reduce-scatter.2.cloned.1.call-update
  229.6 66.3 %reduce-scatter.2.cloned.1.call-done = bf16[16,2432]{1,0:T(8,128)(2,1)} async-done(((bf16[256,2432]{1,0:T(8,128)(2,1)}), bf16[16,2432]{1,0:T(8,128)(2,1)}) %reduce-scatter.2.cloned.1.call-update) | async-done | bytes 77840 | tf_op jit(solution)/shard_map/reduce_scatter | solution.py:139
  295.9 1.1 fusion.49
  297.0 1.7 multiply_reduce_fusion.2
  298.7 0.0 copy-done.5
  298.7 1.2 fusion.36
  299.9 0.1 reshape.194
  300.0 2.6 collective-permute-start
  303.3 1.2 collective-permute-done
  304.6 0.0 copy-done.8
  304.6 0.6 multiply_add_fusion.2
  (37 shorter events, 0.3 us)
Async XLA Ops:
  7.2 214.8 %copy-start = (bf16[608,2432]{1,0:T(8,128)(2,1)S(1)}, bf16[608,2432]{1,0:T(8,128)(2,1)}, u32[]{:S(2)}) copy-start(bf16[608,2432]{1,0:T(8,128)(2,1)} %param.22) | copy-start | bytes 8871940
  7.2 4.9 %copy-start.4 = (bf16[1,154,2,128]{3,2,1,0:T(2,128)(2,1)S(1)}, bf16[1,154,2,128]{3,2,1,0:T(2,128)(2,1)}, u32[]{:S(2)}) copy-start(bf16[1,154,2,128]{3,2,1,0:T(2,128)(2,1)} %param.15) | copy-start | bytes 236548
  7.2 5.9 %copy-start.9 = (f32[2,64]{1,0:T(2,128)S(1)}, f32[2,64]{1,0:T(2,128)}, u32[]{:S(2)}) copy-start(f32[2,64]{1,0:T(2,128)} %param.19) | copy-start | bytes 1540
  7.2 6.0 %copy-start.6 = (f32[1,8,2432]{2,1,0:T(8,128)S(1)}, f32[1,8,2432]{2,1,0:T(8,128)}, u32[]{:S(2)}) copy-start(f32[1,8,2432]{2,1,0:T(8,128)} %param.17) | copy-start | bytes 233476
  7.2 41.0 %all-gather.2.cloned.1.call-start = ((), (), s32[]{:S(2)}) async-start(), calls=%async_computation.1 | async-start | bytes 1323008 | tf_op jit(solution)/shard_map/all_gather | solution.py:59
  7.9 210.0 %all-reduce.2.cloned.1.call-start = ((), (), s32[]{:S(2)}) async-start(), calls=%async_computation.2 | async-start | bytes 2490368 | tf_op jit(solution)/shard_map/psum | solution.py:129
  48.2 3.5 %copy-start.1 = (bf16[1,16,16,2432]{3,2,0,1:T(8,128)(2,1)S(1)}, bf16[1,16,16,2432]{3,2,0,1:T(8,128)(2,1)}, u32[]{:S(2)}) copy-start(bf16[1,16,16,2432]{3,2,0,1:T(8,128)(2,1)} %all-gather.2.cloned.1.call-done) | copy-start | bytes 3735556
  48.2 4.1 %copy-start.3 = (bf16[2432,3,128]{0,2,1:T(8,128)(2,1)S(1)}, bf16[2432,3,128]{0,2,1:T(8,128)(2,1)}, u32[]{:S(2)}) copy-start(bf16[2432,3,128]{0,2,1:T(8,128)(2,1)} %copy.26) | copy-start | bytes 5603332
  93.6 202.3 %reduce-scatter.2.cloned.1.call-start = ((), (), s32[]{:S(2)}) async-start(), calls=%async_computation.3 | async-start | bytes 1323008 | tf_op jit(solution)/shard_map/reduce_scatter | solution.py:139
  220.1 1.4 copy-start.2
  220.2 1.9 copy-start.7
  222.0 76.7 %copy-start.5 = (bf16[2432,64]{0,1:T(8,128)(2,1)S(1)}, bf16[2432,64]{0,1:T(8,128)(2,1)}, u32[]{:S(2)}) copy-start(bf16[2432,64]{0,1:T(8,128)(2,1)} %param.23) | copy-start | bytes 933892
  229.5 75.0 %copy-start.8 = (f32[1,1,1024]{2,1,0:T(1,128)S(1)}, f32[1,1,1024]{2,1,0:T(1,128)}, u32[]{:S(2)}) copy-start(f32[1,1,1024]{2,1,0:T(1,128)} %param.25) | copy-start | bytes 12292
  300.0 4.5 %collective-permute-start = (f32[1,1,1024]{2,1,0:T(1,128)S(1)}, f32[1,1,1024]{2,1,0:T(1,128)S(1)}, u32[]{:S(2)}, u32[]{:S(2)}) collective-permute-start(f32[1,1,1024]{2,1,0:T(1,128)S(1)} %reshape.194), channel_id=1, source_target_pairs={{0,1},{1,0},{2,3},{3,2},{4,5},{5,4},{6,7},{7,6},{8,9},{9,8},{10,11... | collective-permute-start | bytes 12296 | tf_op jit(solution)/shard_map/ppermute | solution.py:17
Sparse Core Ops, SparseCore 0:
  9.9 38.2 all-gather.1
  93.8 124.1 all-reduce.1
  229.7 66.1 reduce-scatter.1
where the time goes:
time: 312 us
  waiting for transfers between devices  227 us (73%)
  blocking collectives  25.6 us (8%)
  matrix products  18 us (6%)
  between operations  15.4 us (5%)
  local copies, waits for them, and re-layouts  11.5 us (4%)
  other arithmetic  11.5 us (4%)
    psum x1, waiting for transfers between devices, on_device(): lax.psum(jnp.dot(attended, output_weight, preferred_element_type=jnp.floa...  124 us
    reduce_scatter x1, waiting for transfers between devices, on_device(): lax.psum_scatter(jnp.dot(hidden, down_weight, preferred_element_type=jnp....  66.3 us
    all_gather x1, waiting for transfers between devices, on_device(): stripe_tokens = lax.all_gather(tokens, 'row', axis=1, tiled=True)  34.3 us
    all_gather x1, blocking collectives, on_device(): value_piece = lax.all_gather(values_image, 'col', axis=0, tiled=True)  13 us
    all_gather x1, blocking collectives, on_device(): key_piece = lax.all_gather(keys_image, 'col', axis=0, tiled=True)  12.6 us
    dot_general x1, matrix products, on_device(): jnp.dot(hidden, down_weight, preferred_element_type=jnp.float32)  7.51 us
  transfers between devices with their start and end apart: 4, of which 4 were waited for; matrix products, arithmetic and copies ran while one was open for 2% of the time, Pallas kernels for 0%

commit v1 on v0

--- a/solution.py
+++ b/solution.py
@@ -112,7 +112,13 @@
         return ((new_max, new_mass, new_sum), None)
 
     key_piece = lax.all_gather(keys_image, "col", axis=0, tiled=True)
-    value_piece = lax.all_gather(values_image, "col", axis=0, tiled=True)
+    n_dev = lax.axis_size("col")
+    held, pieces = (values_image, [values_image])
+    for _ in range(n_dev - 1):
+        held = lax.ppermute(held, "col", [(i, (i + 1) % n_dev) for i in range(n_dev)])
+        pieces.insert(0, held)
+    line = jnp.concatenate(pieces, axis=0)
+    value_piece = jnp.roll(line, (lax.axis_index("col") + 1) * values_image.shape[0], axis=0)
     blocks = key_piece.shape[0] // stripe_rows
     key_blocks = key_piece.reshape(blocks, stripe_rows, local_heads, HD)
     value_blocks = value_piece.reshape(blocks, stripe_rows, local_heads, HD)

time: 312 us -> 313 us (level)
  blocking collectives: 25.6 us -> 13.2 us
  local copies, waits for them, and re-layouts: 11.5 us -> 16.2 us
  waiting for transfers between devices: 227 us -> 231 us
  starting transfers between devices: 2.67 us -> 5.98 us
    all_gather x1 -> x0, blocking collectives: 13 us -> none  [on_device(): value_piece = lax.all_gather(values_image, 'col', axis=0, tiled=True)]
    ppermute x0 -> x3, waiting for transfers between devices: none -> 6.57 us  [on_device(): lax.ppermute(held, 'col', [(i, (i + 1) % n_dev) for i in range(n_dev)])]
    unnamed x21 -> x44, local copies, waits for them, and re-layouts: 5.54 us -> 8.99 us
    dot_general x4, matrix products: 4.33 us -> 0.95 us  [one_block(): jnp.einsum('hsk,khd->hsd', weights.astype(jnp.bfloat16), value_block, pre...]
    dot_general x4, matrix products: 1.15 us -> 4.5 us  [one_block(): jnp.einsum('hsd,khd->hsk', queries, key_block, preferred_element_type=jnp...]
  transfers between devices with their start and end apart: 4 -> 7, of which waited for: 4 -> 6; matrix products, arithmetic and copies ran while one was open for 2% -> 4% of each run, Pallas kernels for 0% -> 0%
where the time goes in v1:
time: 313 us
  waiting for transfers between devices  231 us (74%)
  matrix products  18 us (6%)
  local copies, waits for them, and re-layouts  16.2 us (5%)
  between operations  15.5 us (5%)
  blocking collectives  13.2 us (4%)
  other arithmetic  12.2 us (4%)
  starting transfers between devices  5.98 us (2%)
    psum x1, waiting for transfers between devices, on_device(): lax.psum(jnp.dot(attended, output_weight, preferred_element_type=jnp.floa...  125 us
    reduce_scatter x1, waiting for transfers between devices, on_device(): lax.psum_scatter(jnp.dot(hidden, down_weight, preferred_element_type=jnp....  66.2 us
    all_gather x1, waiting for transfers between devices, on_device(): stripe_tokens = lax.all_gather(tokens, 'row', axis=1, tiled=True)  32.3 us
    all_gather x1, blocking collectives, on_device(): key_piece = lax.all_gather(keys_image, 'col', axis=0, tiled=True)  13.2 us
    unnamed x44, local copies, waits for them, and re-layouts  8.99 us
    dot_general x1, matrix products, on_device(): jnp.dot(hidden, down_weight, preferred_element_type=jnp.float32)  7.51 us
    ppermute x3, waiting for transfers between devices, on_device(): lax.ppermute(held, 'col', [(i, (i + 1) % n_dev) for i in range(n_dev)])  6.57 us
  transfers between devices with their start and end apart: 7, of which 6 were waited for; matrix products, arithmetic and copies ran while one was open for 4% of the time, Pallas kernels for 0%

profile of v1, /device:TPU:8, one launch (start us, length us, event | category | flops | bytes accessed | tf_op | source)
XLA Modules:
  0.0 312.6 jit_solution(13941066035452799763)
XLA Ops:
  7.2 0.0 all-gather.2.cloned.1.call-start
  7.3 0.7 all-gather.2.cloned.1.call-update
  7.9 0.0 all-reduce.2.cloned.1.call-start
  8.0 4.1 %copy.26 = bf16[2432,3,128]{0,2,1:T(8,128)(2,1)} copy(bf16[2432,3,128]{2,0,1:T(8,128)(2,1)} %param.18) | data formatting | bytes 3735552 | tf_op args[4]
  12.1 0.1 fusion.53
  12.2 0.8 copy.27
  13.6 0.7 copy.28
  14.4 0.1 mul.232
  14.5 0.6 iota_compare_fusion
  15.1 0.8 add_reduce_fusion
  15.9 32.3 %all-gather.2.cloned.1.call-done = bf16[1,16,16,2432]{3,2,0,1:T(8,128)(2,1)} async-done(((bf16[1,1,16,2432]{3,2,0,1:T(8,128)(2,1)}), bf16[1,16,16,2432]{3,2,0,1:T(8,128)(2,1)}) %all-gather.2.cloned.1.call-update) | async-done | bytes 1245200 | tf_op jit(solution)/shard_map/all_gather | solution.py:59
  48.2 1.7 convert_reduce_fusion
  49.9 1.7 multiply_reduce_fusion.1
  51.6 0.0 copy-done.1
  51.6 0.6 add_convert_fusion.1
  52.3 0.7 fusion.55
  53.1 1.6 collective-permute-start
  54.7 0.1 fusion.41
  54.8 0.3 fusion.54
  55.0 0.2 fusion.31
  55.2 0.1 fusion.35
  55.3 2.2 collective-permute-done
  57.5 1.5 collective-permute-start.1
  59.0 13.2 %all_gather.7 = bf16[1024,128]{0,1:T(8,128)(2,1)} all-gather(bf16[256,128]{0,1:T(8,128)(2,1)S(1)} %fusion.35), channel_id=1, replica_groups=mesh['row'=16,'col'=4,'item'=4] {'col'}, dimensions={0}, use_global_device_ids=true | all-gather | bytes 327680 | tf_op jit(solution)/shard_map/all_gather | solution.py:114
  72.2 1.8 reshape.190
  74.0 1.7 copy.29
  75.7 0.1 fusion.30
  75.8 4.4 %collective-permute-done.2 = bf16[256,128]{0,1:T(8,128)(2,1)S(1)} collective-permute-done((bf16[256,128]{0,1:T(8,128)(2,1)}, bf16[256,128]{0,1:T(8,128)(2,1)S(1)}, u32[]{:S(2)}, u32[]{:S(2)}) %collective-permute-start.2) | collective-permute-done | bytes 65568 | tf_op jit(solution)/shard_map/ppermute | solution.py:118
  80.2 0.8 constant_dynamic-update-slice_fusion.6
  81.0 0.8 constant_dynamic-update-slice_fusion.5
  81.9 0.8 constant_dynamic-update-slice_fusion.2
  82.8 0.8 constant_dynamic-update-slice_fusion.1
  83.7 0.9 reshape.191
  84.5 1.0 copy.30
  85.5 6.1 %while.14 = (s32[]{:T(128)}, f32[2,256]{1,0:T(2,128)S(1)}, f32[2,256]{1,0:T(2,128)S(1)}, f32[2,256,64]{1,2,0:T(8,128)S(1)}, bf16[4,256,2,64]{1,3,2,0:T(8,128)(2,...) while((s32[]{:T(128)}, f32[2,256]{1,0:T(2,128)S(1)}, ...), condition=%wide.region_9.10_spmd, body=%wide.region_6.9_spmd.sunk | while | flops 34407424 | bytes 2064985 | solution.py:125
  85.5 1.1 fusion.75
  86.7 0.1 fusion.76
  86.8 0.2 convolution_add_fusion.2
  87.1 1.1 fusion.75
  88.2 0.1 fusion.76
  88.3 0.2 convolution_add_fusion.2
  88.6 1.1 fusion.75
  89.7 0.1 fusion.76
  89.8 0.2 convolution_add_fusion.2
  90.1 1.1 fusion.75
  91.3 0.1 fusion.76
  91.4 0.2 convolution_add_fusion.2
  91.7 2.7 convolution_convert_fusion
  94.3 0.0 all-reduce.2.cloned.1.call-update
  94.3 0.0 reduce-scatter.2.cloned.1.call-start
  94.4 124.6 %all-reduce.2.cloned.1.call-done = bf16[256,2432]{1,0:T(8,128)(2,1)} async-done(((bf16[256,2432]{1,0:T(8,128)(2,1)}), bf16[256,2432]{1,0:T(8,128)(2,1)}) %all-reduce.2.cloned.1.call-update) | async-done | bytes 1245200 | tf_op jit(solution)/shard_map/psum | solution.py:135
  219.0 2.2 fusion.51
  221.2 1.4 copy-done.2
  222.6 0.4 multiply_reduce_fusion
  223.0 7.5 %convolution_convert_fusion.1 = bf16[256,2432]{1,0:T(8,128)(2,1)} fusion(bf16[608,2432]{1,0:T(8,128)(2,1)S(1)} %copy-done, bf16[2432,608]{0,1:T(8,128)(2,1)} %param.21, f32[256,2432]{1,0:T(8,128)} %copy-done.2, f32[2432]{0:T(1024)S(1)} %copy-done.13, f32[2432]{0:T(1024)S(1)} %copy-done.14, f32[256]{0:T(256)S(1)} %add_rsqrt_fusion.3, ...), kind=kOutput, calls=%fused_computation.16 | convolution fusion | flops 1519280128 | bytes 9671680 | tf_op jit(solution)/shard_map/dot_general | solution.py:146
  230.6 0.0 reduce-scatter.2.cloned.1.call-update
  230.6 66.2 %reduce-scatter.2.cloned.1.call-done = bf16[16,2432]{1,0:T(8,128)(2,1)} async-done(((bf16[256,2432]{1,0:T(8,128)(2,1)}), bf16[16,2432]{1,0:T(8,128)(2,1)}) %reduce-scatter.2.cloned.1.call-update) | async-done | bytes 77840 | tf_op jit(solution)/shard_map/reduce_scatter | solution.py:145
  296.7 1.1 fusion.49
  297.8 1.7 multiply_reduce_fusion.2
  299.6 1.2 fusion.36
  300.8 0.1 reshape.194
  300.9 2.7 collective-permute-start.3
  304.4 1.1 collective-permute-done.3
  305.4 0.6 multiply_add_fusion.2
  (67 shorter events, 0.4 us)
Async XLA Ops:
  7.2 215.8 %copy-start = (bf16[608,2432]{1,0:T(8,128)(2,1)S(1)}, bf16[608,2432]{1,0:T(8,128)(2,1)}, u32[]{:S(2)}) copy-start(bf16[608,2432]{1,0:T(8,128)(2,1)} %param.22) | copy-start | bytes 8871940
  7.2 4.9 %copy-start.4 = (bf16[1,154,2,128]{3,2,1,0:T(2,128)(2,1)S(1)}, bf16[1,154,2,128]{3,2,1,0:T(2,128)(2,1)}, u32[]{:S(2)}) copy-start(bf16[1,154,2,128]{3,2,1,0:T(2,128)(2,1)} %param.15) | copy-start | bytes 236548
  7.2 7.2 %copy-start.16 = (f32[2,64]{1,0:T(2,128)S(1)}, f32[2,64]{1,0:T(2,128)}, u32[]{:S(2)}) copy-start(f32[2,64]{1,0:T(2,128)} %param.19) | copy-start | bytes 1540
  7.2 7.9 %copy-start.9 = (f32[1,8,2432]{2,1,0:T(8,128)S(1)}, f32[1,8,2432]{2,1,0:T(8,128)}, u32[]{:S(2)}) copy-start(f32[1,8,2432]{2,1,0:T(8,128)} %param.17) | copy-start | bytes 233476
  7.2 41.0 %all-gather.2.cloned.1.call-start = ((), (), s32[]{:S(2)}) async-start(), calls=%async_computation.1 | async-start | bytes 1323008 | tf_op jit(solution)/shard_map/all_gather | solution.py:59
  7.9 211.0 %all-reduce.2.cloned.1.call-start = ((), (), s32[]{:S(2)}) async-start(), calls=%async_computation.2 | async-start | bytes 2490368 | tf_op jit(solution)/shard_map/psum | solution.py:135
  48.2 3.5 %copy-start.1 = (bf16[1,16,16,2432]{3,2,0,1:T(8,128)(2,1)S(1)}, bf16[1,16,16,2432]{3,2,0,1:T(8,128)(2,1)}, u32[]{:S(2)}) copy-start(bf16[1,16,16,2432]{3,2,0,1:T(8,128)(2,1)} %all-gather.2.cloned.1.call-done) | copy-start | bytes 3735556
  48.2 4.1 %copy-start.3 = (bf16[2432,3,128]{0,2,1:T(8,128)(2,1)S(1)}, bf16[2432,3,128]{0,2,1:T(8,128)(2,1)}, u32[]{:S(2)}) copy-start(bf16[2432,3,128]{0,2,1:T(8,128)(2,1)} %copy.26) | copy-start | bytes 5603332
  52.2 2.5 copy-start.6
  52.3 2.5 copy-start.17
  52.3 2.8 copy-start.7
  53.1 4.4 %collective-permute-start = (bf16[256,128]{0,1:T(8,128)(2,1)S(1)}, bf16[256,128]{0,1:T(8,128)(2,1)}, u32[]{:S(2)}, u32[]{:S(2)}) collective-permute-start(bf16[256,128]{0,1:T(8,128)(2,1)S(1)} %bitcast.81), channel_id=1, source_target_pairs={{0,4},{4,8},{8,12},{12,0},{1,5},{5,9},{9,13},{13,1},{2,6},{6,10},{... | collective-permute-start | bytes 196616 | tf_op jit(solution)/shard_map/ppermute | solution.py:118
  57.5 18.2 %collective-permute-start.1 = (bf16[256,128]{0,1:T(8,128)(2,1)}, bf16[256,128]{0,1:T(8,128)(2,1)}, u32[]{:S(2)}, u32[]{:S(2)}) collective-permute-start(bf16[256,128]{0,1:T(8,128)(2,1)} %collective-permute-done), channel_id=1, source_target_pairs={{0,4},{4,8},{8,12},{12,0},{1,5},{5,9},{9,13},{13,1},{2,6},{6,10},{... | collective-permute-start | bytes 196616 | tf_op jit(solution)/shard_map/ppermute | solution.py:118
  75.7 4.5 %collective-permute-start.2 = (bf16[256,128]{0,1:T(8,128)(2,1)}, bf16[256,128]{0,1:T(8,128)(2,1)S(1)}, u32[]{:S(2)}, u32[]{:S(2)}) collective-permute-start(bf16[256,128]{0,1:T(8,128)(2,1)} %collective-permute-done.1), channel_id=1, source_target_pairs={{0,4},{4,8},{8,12},{12,0},{1,5},{5,9},{9,13},{13,1},{2,6},{6,10},{... | collective-permute-start | bytes 196616 | tf_op jit(solution)/shard_map/ppermute | solution.py:118
  91.6 127.3 %copy-start.10 = (f32[2432]{0:T(1024)S(1)}, f32[2432]{0:T(1024)}, u32[]{:S(2)}) copy-start(f32[2432]{0:T(1024)} %get-tuple-element.63) | copy-start | bytes 29188
  94.3 202.4 %reduce-scatter.2.cloned.1.call-start = ((), (), s32[]{:S(2)}) async-start(), calls=%async_computation.3 | async-start | bytes 1323008 | tf_op jit(solution)/shard_map/reduce_scatter | solution.py:145
  221.1 1.4 copy-start.2
  221.1 1.9 copy-start.13
  221.1 1.9 copy-start.14
  223.0 73.7 %copy-start.8 = (f32[2432]{0:T(1024)S(1)}, f32[2432]{0:T(1024)}, u32[]{:S(2)}) copy-start(f32[2432]{0:T(1024)} %get-tuple-element.60) | copy-start | bytes 29188
  223.0 76.6 %copy-start.5 = (bf16[2432,64]{0,1:T(8,128)(2,1)S(1)}, bf16[2432,64]{0,1:T(8,128)(2,1)}, u32[]{:S(2)}) copy-start(bf16[2432,64]{0,1:T(8,128)(2,1)} %param.23) | copy-start | bytes 933892
  223.0 76.6 %copy-start.11 = (f32[2432]{0:T(1024)S(1)}, f32[2432]{0:T(1024)}, u32[]{:S(2)}) copy-start(f32[2432]{0:T(1024)} %get-tuple-element.57) | copy-start | bytes 29188
  223.0 76.6 %copy-start.12 = (f32[2432]{0:T(1024)S(1)}, f32[2432]{0:T(1024)}, u32[]{:S(2)}) copy-start(f32[2432]{0:T(1024)} %get-tuple-element.64) | copy-start | bytes 29188
  230.6 74.9 %copy-start.15 = (f32[1,1,1024]{2,1,0:T(1,128)S(1)}, f32[1,1,1024]{2,1,0:T(1,128)}, u32[]{:S(2)}) copy-start(f32[1,1,1024]{2,1,0:T(1,128)} %param.25) | copy-start | bytes 12292
  300.9 4.5 %collective-permute-start.3 = (f32[1,1,1024]{2,1,0:T(1,128)S(1)}, f32[1,1,1024]{2,1,0:T(1,128)S(1)}, u32[]{:S(2)}, u32[]{:S(2)}) collective-permute-start(f32[1,1,1024]{2,1,0:T(1,128)S(1)} %reshape.194), channel_id=1, source_target_pairs={{0,1},{1,0},{2,3},{3,2},{4,5},{5,4},{6,7},{7,6},{8,9},{9,8},{10,11... | collective-permute-start | bytes 12296 | tf_op jit(solution)/shard_map/ppermute | solution.py:17
Sparse Core Ops, SparseCore 0:
  9.9 38.2 all-gather.1
  94.5 124.4 all-reduce.1
  230.7 65.9 reduce-scatter.1
